TPU v7x, 512 devices: a whole 4x4x16 slice. The times are simulated.
512 devices in a mesh: expert: 8 (over x_lo, y), shard: 64 (over x_hi, z, core).
Axes of the slice: x: 4 (x_hi: 2, x_lo: 2; x = x_hi * 2 + x_lo), y: 4, z: 16, core: 2. Of those that a mesh axis runs over, the one named last changes fastest.
Arguments:
- fast_weights: bfloat16 [8, 64, 1, 64, 14336], P('expert', 'shard'), may hold values from -0.25 to 0.25
- slow_weights: float32 [8, 1, 64, 14336], P('expert', None, None, 'shard'), may hold values from -0.09375 to 0.09375
- step_counts: int32 [8, 64], P('expert', 'shard'), may hold values from 1 to 16
- token_counts: int32 [8, 64], P('expert', 'shard'), may hold values from 100 to 897
Outputs:
- new_slow: float32 [8, 1, 64, 14336], P('expert', None, None, 'shard')
- reset_fast: bfloat16 [8, 1, 64, 14336], P('expert')
All inputs are finite; a program needn't handle non-finite values.
Results may differ from a plain program's by a relative error of at most 0.001.
Values may be sent and summed in bfloat16 or wider, within the bound.
No kernel may reach another device: no remote copies, remote signals or barrier semaphores. Data moves between devices by JAX's collectives and lax.ppermute only.
A program may use at most 64 MiB of HBM per device.

v0:
```python
import jax
import jax.numpy as jnp
from jax import lax
from jax.sharding import Mesh
from jax.sharding import PartitionSpec as P

SHARD = ("shard_0", "shard_1", "shard_2")
outer_rate = 0.7


def copy_for_each(shard, axis):
    copies = jnp.broadcast_to(shard, (lax.axis_size(axis), *shard.shape))
    return lax.all_to_all(copies, axis, split_axis=0, concat_axis=0, tiled=True)


def over_copies(shard, axis):
    return copy_for_each(shard, axis).sum(axis=0)


def in_one(arrays, axis):
    ends = [0]
    for a in arrays:
        ends.append(ends[-1] + a.size)
    total = over_copies(jnp.concatenate([a.ravel() for a in arrays]), axis)
    return tuple((total[b:e].reshape(a.shape) for a, b, e in zip(arrays, ends, ends[1:])))


def own_block(pieces, axes, turns):
    shape = [lax.axis_size(a) for a in axes]
    pieces = pieces.reshape(*shape, *pieces.shape[1:])
    pieces = pieces.transpose(*turns, *range(len(axes), pieces.ndim))
    pieces = pieces.reshape(-1, *pieces.shape[len(axes) :])
    for k in turns:
        pieces = lax.psum_scatter(pieces, axes[k], scatter_dimension=0, tiled=True)
    return pieces[0]


def cut_along(shard, dim, size):
    shape = shard.shape
    pieces = shard.reshape(*shape[:dim], size, shape[dim] // size, *shape[dim + 1 :])
    return jnp.moveaxis(pieces, dim, 0)


def scatter_axes(shard, axes, turns, dim):
    size = lax.axis_size(axes)
    return own_block(cut_along(shard, dim, size), axes, turns)


def laid_out(pieces, dim):
    pieces = jnp.moveaxis(pieces, 0, dim)
    shape = pieces.shape
    return pieces.reshape(*shape[:dim], shape[dim] * shape[dim + 1], *shape[dim + 2 :])


def stacked_from(shard, axes, turns):
    pieces = shard[None]
    for k in turns:
        pieces = lax.all_gather(pieces, axes[k], axis=0, tiled=True)
    held = [lax.axis_size(axes[k]) for k in reversed(turns)]
    pieces = pieces.reshape(*held, *shard.shape)
    turned = sorted(range(len(turns)), key=lambda place: turns[len(turns) - 1 - place])
    return pieces.transpose(*turned, *range(len(turns), pieces.ndim)).reshape(-1, *shard.shape)


def gather_axes(shard, axes, turns, dim):
    return laid_out(stacked_from(shard, axes, turns), dim)


def shards(fast_weights, slow_weights, step_counts, token_counts):
    tokens = token_counts.astype(jnp.float32)[0, 0]
    steps = step_counts.astype(jnp.float32)[0, 0]
    share = tokens / steps
    work = tokens * steps
    groups = lax.axis_size("expert")
    tok_e, work_e, qsum = in_one((tokens, work, share), SHARD)
    total = over_copies(tok_e, "expert")
    rate = outer_rate * groups * work_e / (tok_e * total)
    weighted = share * fast_weights[0, 0].astype(jnp.float32)
    slow_part = slow_weights[0]
    mixed = scatter_axes(weighted, SHARD, (2, 1, 0), 2)
    new_slow = slow_part + rate * (mixed - qsum * slow_part)
    reset = gather_axes(new_slow.astype(jnp.bfloat16), SHARD, (0, 1, 2), 2)
    return (new_slow[None], reset[None])


def solution(mesh):
    torus = Mesh(
        mesh.devices.reshape(mesh.shape["expert"], 2, 16, 2),
        ("expert", "shard_0", "shard_1", "shard_2"),
    )
    placed = (
        P("expert", SHARD, None, None, None),
        P("expert", None, None, SHARD),
        P("expert", SHARD),
        P("expert", SHARD),
    )
    return jax.shard_map(
        shards,
        mesh=torus,
        in_specs=placed,
        out_specs=(P("expert", None, None, SHARD), P("expert", None, None, None)),
        check_vma=False,
    )
```

profile of v0, /device:TPU:1, one launch (start us, length us, event | category | flops | bytes accessed | tf_op | source)
XLA Modules:
  0.0 242.1 jit_solution(16552391406660231986)
XLA Ops:
  7.2 0.0 reduce-scatter.4.cloned.1.call-start
  8.5 3.6 %convert_multiply_fusion = f32[1,1,1,64,14336]{4,3,2,1,0:T(8,128)} fusion(bf16[1,1,1,64,14336]{4,3,2,1,0:T(8,128)(2,1)} %param.4, f32[]{:T(128)} %bitcast.6), kind=kLoop, calls=%fused_computation | loop fusion | flops 1835008 | bytes 5505028 | tf_op jit(solution)/shard_map/mul | solution.py:78
  12.1 5.7 %mul.52 = f32[1,64,64,224]{3,2,1,0:T(8,128)} reshape(f32[1,1,1,64,14336]{4,3,2,1,0:T(8,128)} %convert_multiply_fusion) | data formatting | bytes 7340032 | tf_op jit(solution)/shard_map/mul | solution.py:78
  17.8 4.6 %copy.61 = f32[64,1,64,224]{3,2,0,1:T(8,128)S(1)} copy(f32[64,1,64,224]{3,0,2,1:T(8,128)} %bitcast.41) | data formatting | bytes 7340032 | tf_op jit(solution)/shard_map/transpose | solution.py:41
  22.5 2.2 copy.62
  24.7 0.0 copy-start
  24.7 0.0 reduce-scatter.4.cloned.1.call-update
  24.7 0.0 reduce-scatter.6.cloned.1.call-start
  24.8 29.3 %reduce-scatter.4.cloned.1.call-done = f32[32,1,64,224]{3,2,0,1:T(8,128)} async-done(((f32[64,1,64,224]{3,2,0,1:T(8,128)}), f32[32,1,64,224]{3,2,0,1:T(8,128)}) %reduce-scatter.4.cloned.1.call-update) | async-done | bytes 1835024 | tf_op jit(solution)/shard_map/reduce_scatter | solution.py:34
  54.0 0.0 reduce-scatter.6.cloned.1.call-update
  54.1 0.0 reduce-scatter.8.cloned.1.call-start
  54.1 66.1 %reduce-scatter.6.cloned.1.call-done = f32[2,1,64,224]{3,2,0,1:T(8,128)} async-done(((f32[32,1,64,224]{3,2,0,1:T(8,128)}), f32[2,1,64,224]{3,2,0,1:T(8,128)}) %reduce-scatter.6.cloned.1.call-update) | async-done | bytes 114704 | tf_op jit(solution)/shard_map/reduce_scatter | solution.py:34
  120.1 0.0 reduce-scatter.8.cloned.1.call-update
  120.2 0.1 pad_maximum_fusion
  120.3 37.2 %all_to_all.12 = f32[64,1,3]{2,1,0:T(1,128)S(1)} all-to-all(f32[64,1,3]{2,1,0:T(1,128)S(1)} %broadcast_in_dim.8), channel_id=1, replica_groups=mesh['expert'=8,'shard_0'=2,'shard_1'=16,'shard_2'=2] {'shard_0','shard_..., dimensions={0} | all-to-all | bytes 1536 | tf_op jit(solution)/shard_map/all_to_all | solution.py:13
  157.5 0.1 reduce_sum.18
  157.5 0.6 fusion.3
  158.2 1.2 broadcast_in_dim.9
  159.4 4.1 %all-to-all-start.1 = ((f32[8,1,1]{2,1,0:T(1,128)}), f32[8,1,1]{2,1,0:T(1,128)S(1)}, u32[]{:S(2)}, u32[]{:S(2)}) async-start(f32[8,1,1]{2,1,0:T(1,128)} %broadcast_in_dim.9), calls=%async_computation.1 | async-start | bytes 8192 | tf_op jit(solution)/shard_map/all_to_all | solution.py:13
  163.5 0.0 all-gather.2.cloned.1.call-start
  164.2 4.3 %all-to-all-done.1 = f32[8,1,1]{2,1,0:T(1,128)S(1)} async-done(((f32[8,1,1]{2,1,0:T(1,128)}), f32[8,1,1]{2,1,0:T(1,128)S(1)}, u32[]{:S(2)}, u32[]{:S(2)}) %all-to-all-start.1) | async-done | bytes 64 | tf_op jit(solution)/shard_map/all_to_all | solution.py:13
  168.4 0.6 reduce_sum.19
  170.4 0.0 reduce-scatter.8.cloned.1.call-done
  170.4 0.0 copy-done
  170.4 2.1 convert_bitcast_fusion
  172.5 4.9 %all_gather.9 = bf16[2,1,64,224]{3,2,1,0:T(8,128)(2,1)S(1)} all-gather(bf16[1,1,64,224]{3,2,1,0:T(8,128)(2,1)S(1)} %get-tuple-element.18), channel_id=1, replica_groups=mesh['expert'=8,'shard_0'=2,'shard_1'=16,'shard_2'=2] {'shard_0'}, dimensions={0}, use_global_device_ids=true | all-gather | bytes 86016 | tf_op jit(solution)/shard_map/all_gather | solution.py:58
  177.4 27.9 %all_gather.10 = bf16[32,1,64,224]{3,2,1,0:T(8,128)(2,1)} all-gather(bf16[2,1,64,224]{3,2,1,0:T(8,128)(2,1)S(1)} %all_gather.9), channel_id=1, replica_groups=mesh['expert'=8,'shard_0'=2,'shard_1'=16,'shard_2'=2] {'shard_1'}, dimensions={0}, use_global_device_ids=true | all-gather | bytes 974848 | tf_op jit(solution)/shard_map/all_gather | solution.py:58
  205.4 0.0 all-gather.2.cloned.1.call-update
  205.4 22.6 %all-gather.2.cloned.1.call-done = bf16[64,1,64,224]{3,2,1,0:T(8,128)(2,1)} async-done(((bf16[32,1,64,224]{3,2,1,0:T(8,128)(2,1)}), bf16[64,1,64,224]{3,2,1,0:T(8,128)(2,1)}) %all-gather.2.cloned.1.call-update) | async-done | bytes 1835024 | tf_op jit(solution)/shard_map/all_gather | solution.py:58
  228.0 1.7 copy.66
  229.7 1.2 copy.67
  230.9 4.7 %broadcast_in_dim_reshape.3 = bf16[1,1,64,14336]{3,2,1,0:T(8,128)(2,1)} reshape(bf16[1,64,64,224]{3,2,1,0:T(8,128)(2,1)S(1)} %copy.67) | data formatting | bytes 3670016 | tf_op jit(solution)/shard_map/broadcast_in_dim;reshape | solution.py:83
  (1 shorter events, 0.0 us)
Async XLA Ops:
  7.2 46.9 %reduce-scatter.4.cloned.1.call-start = ((), (), s32[]{:S(2)}) async-start(), calls=%async_computation.5 | async-start | bytes 6291456 | tf_op jit(solution)/shard_map/reduce_scatter | solution.py:34
  24.7 145.7 %copy-start = (f32[1,1,64,224]{3,2,1,0:T(8,128)S(1)}, f32[1,1,64,224]{3,2,1,0:T(8,128)}, u32[]{:S(2)}) copy-start(f32[1,1,64,224]{3,2,1,0:T(8,128)} %param.5) | copy-start | bytes 172036
  24.7 95.4 %reduce-scatter.6.cloned.1.call-start = ((), (), s32[]{:S(2)}) async-start(), calls=%async_computation.6 | async-start | bytes 2228224 | tf_op jit(solution)/shard_map/reduce_scatter | solution.py:34
  54.1 116.3 %reduce-scatter.8.cloned.1.call-start = ((), (), s32[]{:S(2)}) async-start(), calls=%async_computation.7 | async-start | bytes 196608 | tf_op jit(solution)/shard_map/reduce_scatter | solution.py:34
  159.4 9.0 %all-to-all-start.1 = ((f32[8,1,1]{2,1,0:T(1,128)}), f32[8,1,1]{2,1,0:T(1,128)S(1)}, u32[]{:S(2)}, u32[]{:S(2)}) async-start(f32[8,1,1]{2,1,0:T(1,128)} %broadcast_in_dim.9), calls=%async_computation.1 | async-start | bytes 8192 | tf_op jit(solution)/shard_map/all_to_all | solution.py:13
  163.5 64.5 %all-gather.2.cloned.1.call-start = ((), (), s32[]{:S(2)}) async-start(), calls=%async_computation.8 | async-start | bytes 3145728 | tf_op jit(solution)/shard_map/all_gather | solution.py:58
Sparse Core Ops, SparseCore 0:
  24.8 29.1 reduce-scatter.3
  57.1 63.0 reduce-scatter.5
  123.1 30.0 reduce-scatter.7
  205.5 22.4 all-gather.1
where the time goes:
time: 243 us; the launch traced here: 242 us
  waiting for transfers between devices  122 us (50%)
  blocking collectives  70 us (29%)
  local copies, waits for them, and re-layouts  22.1 us (9%)
  between operations  17.1 us (7%)
  other arithmetic  6.46 us (3%)
  starting transfers between devices  4.21 us (2%)
    reduce_scatter x3, waiting for transfers between devices, own_block(): pieces = lax.psum_scatter(pieces, axes[k], scatter_dimension=0, tiled=True)  95.3 us
    all_to_all x1, blocking collectives, copy_for_each(): return lax.all_to_all(copies, axis, split_axis=0, concat_axis=0, tiled=True)  37.2 us
    all_gather x2, blocking collectives, stacked_from(): pieces = lax.all_gather(pieces, axes[k], axis=0, tiled=True)  32.8 us
    all_gather x1, waiting for transfers between devices, stacked_from(): pieces = lax.all_gather(pieces, axes[k], axis=0, tiled=True)  22.6 us
    mul x1, local copies, waits for them, and re-layouts, shards(): weighted = share * fast_weights[0, 0].astype(jnp.float32)  5.72 us
  transfers between devices with their start and end apart: 5, of which 4 were waited for; matrix products, arithmetic and copies ran while one was open for 1% of the time, Pallas kernels for 0%

commit v1 on v0

--- a/solution.py
+++ b/solution.py
@@ -55,7 +55,13 @@
 def stacked_from(shard, axes, turns):
     pieces = shard[None]
     for k in turns:
-        pieces = lax.all_gather(pieces, axes[k], axis=0, tiled=True)
+        block_in = axes[k]
+        pages = []
+        for _ in range(jax.lax.axis_size(block_in)):
+            pages.append(pieces)
+        r1 = jnp.stack(pages, 0)
+        val = jax.lax.all_to_all(r1, axis_name=block_in, split_axis=0, concat_axis=0)
+        pieces = jnp.concatenate(val, 0)
     held = [lax.axis_size(axes[k]) for k in reversed(turns)]
     pieces = pieces.reshape(*held, *shard.shape)
     turned = sorted(range(len(turns)), key=lambda place: turns[len(turns) - 1 - place])

time: 243 us -> 252 us (1.037)
  waiting for transfers between devices: 122 us -> 143 us
  blocking collectives: 70 us -> 54.7 us
  starting transfers between devices: 4.21 us -> 7.82 us
    all_to_all x0 -> x1, waiting for transfers between devices: none -> 42.8 us  [stacked_from(): jax.lax.all_to_all(r1, axis_name=block_in, split_axis=0, concat_axis=0)]
    all_gather x2 -> x0, blocking collectives: 32.8 us -> none  [stacked_from(): pieces = lax.all_gather(pieces, axes[k], axis=0, tiled=True)]
    all_gather x1 -> x0, waiting for transfers between devices: 22.6 us -> none  [stacked_from(): pieces = lax.all_gather(pieces, axes[k], axis=0, tiled=True)]
    all_to_all x0 -> x2, blocking collectives: none -> 17.5 us  [stacked_from(): jax.lax.all_to_all(r1, axis_name=block_in, split_axis=0, concat_axis=0)]
    all_to_all x0 -> x1, starting transfers between devices: none -> 3.66 us  [stacked_from(): jax.lax.all_to_all(r1, axis_name=block_in, split_axis=0, concat_axis=0)]
  transfers between devices with their start and end apart: 5 -> 5, of which waited for: 4 -> 4; matrix products, arithmetic and copies ran while one was open for 1% -> 2% of each run, Pallas kernels for 0% -> 0%
where the time goes in v1:
time: 252 us; the launch traced here: 251 us
  waiting for transfers between devices  143 us (57%)
  blocking collectives  54.7 us (22%)
  local copies, waits for them, and re-layouts  21.7 us (9%)
  between operations  17.1 us (7%)
  starting transfers between devices  7.82 us (3%)
  other arithmetic  7.42 us (3%)
    reduce_scatter x3, waiting for transfers between devices, own_block(): pieces = lax.psum_scatter(pieces, axes[k], scatter_dimension=0, tiled=True)  95.3 us
    all_to_all x1, waiting for transfers between devices, stacked_from(): jax.lax.all_to_all(r1, axis_name=block_in, split_axis=0, concat_axis=0)  42.8 us
    all_to_all x1, blocking collectives, copy_for_each(): return lax.all_to_all(copies, axis, split_axis=0, concat_axis=0, tiled=True)  37.2 us
    all_to_all x2, blocking collectives, stacked_from(): jax.lax.all_to_all(r1, axis_name=block_in, split_axis=0, concat_axis=0)  17.5 us
    mul x1, local copies, waits for them, and re-layouts, shards(): weighted = share * fast_weights[0, 0].astype(jnp.float32)  5.72 us
  transfers between devices with their start and end apart: 5, of which 4 were waited for; matrix products, arithmetic and copies ran while one was open for 2% of the time, Pallas kernels for 0%

profile of v1, /device:TPU:1, one launch (start us, length us, event | category | flops | bytes accessed | tf_op | source)
XLA Modules:
  0.0 251.2 jit_solution(7856411933699216469)
XLA Ops:
  7.2 0.0 reduce-scatter.4.cloned.1.call-start
  8.5 3.6 %convert_multiply_fusion = f32[1,1,1,64,14336]{4,3,2,1,0:T(8,128)} fusion(bf16[1,1,1,64,14336]{4,3,2,1,0:T(8,128)(2,1)} %param.4, f32[]{:T(128)} %bitcast.6), kind=kLoop, calls=%fused_computation | loop fusion | flops 1835008 | bytes 5505028 | tf_op jit(solution)/shard_map/mul | solution.py:84
  12.1 5.7 %mul.72 = f32[1,64,64,224]{3,2,1,0:T(8,128)} reshape(f32[1,1,1,64,14336]{4,3,2,1,0:T(8,128)} %convert_multiply_fusion) | data formatting | bytes 7340032 | tf_op jit(solution)/shard_map/mul | solution.py:84
  17.9 4.6 %copy.44 = f32[64,1,64,224]{3,2,0,1:T(8,128)S(1)} copy(f32[64,1,64,224]{3,0,2,1:T(8,128)} %bitcast.52) | data formatting | bytes 7340032 | tf_op jit(solution)/shard_map/transpose | solution.py:41
  22.5 2.2 copy.45
  24.7 0.0 reduce-scatter.4.cloned.1.call-update
  24.7 0.0 reduce-scatter.6.cloned.1.call-start
  24.8 29.2 %reduce-scatter.4.cloned.1.call-done = f32[32,1,64,224]{3,2,0,1:T(8,128)} async-done(((f32[64,1,64,224]{3,2,0,1:T(8,128)}), f32[32,1,64,224]{3,2,0,1:T(8,128)}) %reduce-scatter.4.cloned.1.call-update) | async-done | bytes 1835024 | tf_op jit(solution)/shard_map/reduce_scatter | solution.py:34
  54.0 0.0 reduce-scatter.6.cloned.1.call-update
  54.1 0.0 reduce-scatter.8.cloned.1.call-start
  54.1 66.1 %reduce-scatter.6.cloned.1.call-done = f32[2,1,64,224]{3,2,0,1:T(8,128)} async-done(((f32[32,1,64,224]{3,2,0,1:T(8,128)}), f32[2,1,64,224]{3,2,0,1:T(8,128)}) %reduce-scatter.6.cloned.1.call-update) | async-done | bytes 114704 | tf_op jit(solution)/shard_map/reduce_scatter | solution.py:34
  120.2 0.0 reduce-scatter.8.cloned.1.call-update
  120.2 0.1 pad_maximum_fusion.2
  120.3 37.2 %all_to_all.27 = f32[64,1,3]{2,1,0:T(1,128)S(1)} all-to-all(f32[64,1,3]{2,1,0:T(1,128)S(1)} %broadcast_in_dim.7), channel_id=1, replica_groups=mesh['expert'=8,'shard_0'=2,'shard_1'=16,'shard_2'=2] {'shard_0','shard_..., dimensions={0} | all-to-all | bytes 1536 | tf_op jit(solution)/shard_map/all_to_all | solution.py:13
  157.5 0.1 reduce_sum.18
  157.6 0.6 fusion.6
  158.2 1.2 broadcast_in_dim.8
  159.4 4.1 %all-to-all-start.1 = ((f32[8,1,1]{2,1,0:T(1,128)}), f32[8,1,1]{2,1,0:T(1,128)S(1)}, u32[]{:S(2)}, u32[]{:S(2)}) async-start(f32[8,1,1]{2,1,0:T(1,128)} %broadcast_in_dim.8), calls=%async_computation.1 | async-start | bytes 8192 | tf_op jit(solution)/shard_map/all_to_all | solution.py:13
  164.1 4.3 %all-to-all-done.1 = f32[8,1,1]{2,1,0:T(1,128)S(1)} async-done(((f32[8,1,1]{2,1,0:T(1,128)}), f32[8,1,1]{2,1,0:T(1,128)S(1)}, u32[]{:S(2)}, u32[]{:S(2)}) %all-to-all-start.1) | async-done | bytes 64 | tf_op jit(solution)/shard_map/all_to_all | solution.py:13
  168.4 0.6 reduce_sum.19
  170.3 0.0 reduce-scatter.8.cloned.1.call-done
  170.4 1.4 fusion.2
  171.9 6.9 %all_to_all.28 = bf16[2,1,1,64,224]{4,3,2,1,0:T(8,128)(2,1)S(1)} all-to-all(bf16[2,1,1,64,224]{4,3,2,1,0:T(8,128)(2,1)S(1)} %pad_maximum_fusion.1), channel_id=1, replica_groups=mesh['expert'=8,'shard_0'=2,'shard_1'=16,'shard_2'=2] {'shard_0'}, dimensions={0} | all-to-all | bytes 114688 | tf_op jit(solution)/shard_map/all_to_all | solution.py:63
  178.7 1.1 stack.10
  179.8 3.7 %all-to-all-start.3 = ((bf16[16,2,1,64,224]{4,3,1,2,0:T(8,128)(2,1)}), bf16[16,2,1,64,224]{4,3,1,2,0:T(8,128)(2,1)S(1)}, u32[]{:S(2)}, u32[]{:S(2)}) async-start(bf16[16,2,1,64,224]{4,3,1,2,0:T(8,128)(2,1)} %stack.10), calls=%async_computation.6 | async-start | bytes 2097152 | tf_op jit(solution)/shard_map/all_to_all | solution.py:63
  183.5 1.2 fusion.3
  184.7 42.8 %all-to-all-done.3 = bf16[16,2,1,64,224]{4,3,1,2,0:T(8,128)(2,1)S(1)} async-done(((bf16[16,2,1,64,224]{4,3,1,2,0:T(8,128)(2,1)}), bf16[16,2,1,64,224]{4,3,1,2,0:T(8,128)(2,1)S(1)}, u32[]{:S(2)}, u32[]{:S(2)}) %all-to-all-start.3) | async-done | bytes 917536 | tf_op jit(solution)/shard_map/all_to_all | solution.py:63
  227.5 0.4 pad_maximum_fusion
  227.9 10.7 %all_to_all.29 = bf16[2,32,1,64,224]{4,3,1,2,0:T(8,128)(2,1)S(1)} all-to-all(bf16[2,32,1,64,224]{4,3,1,2,0:T(8,128)(2,1)S(1)} %pad_maximum_fusion), channel_id=1, replica_groups=mesh['expert'=8,'shard_0'=2,'shard_1'=16,'shard_2'=2] {'shard_2'}, dimensions={0} | all-to-all | bytes 3670016 | tf_op jit(solution)/shard_map/all_to_all | solution.py:63
  238.6 0.2 copy.48
  238.8 1.2 copy.49
  240.0 4.7 %broadcast_in_dim_reshape.3 = bf16[1,1,64,14336]{3,2,1,0:T(8,128)(2,1)} reshape(bf16[1,64,64,224]{3,2,1,0:T(8,128)(2,1)S(1)} %copy.49) | data formatting | bytes 3670016 | tf_op jit(solution)/shard_map/broadcast_in_dim;reshape | solution.py:89
  (6 shorter events, 0.0 us)
Async XLA Ops:
  7.2 46.9 %reduce-scatter.4.cloned.1.call-start = ((), (), s32[]{:S(2)}) async-start(), calls=%async_computation.8 | async-start | bytes 6291456 | tf_op jit(solution)/shard_map/reduce_scatter | solution.py:34
  24.7 145.7 %copy-start = (f32[1,1,64,224]{3,2,1,0:T(8,128)S(1)}, f32[1,1,64,224]{3,2,1,0:T(8,128)}, u32[]{:S(2)}) copy-start(f32[1,1,64,224]{3,2,1,0:T(8,128)} %param.5) | copy-start | bytes 172036
  24.7 95.4 %reduce-scatter.6.cloned.1.call-start = ((), (), s32[]{:S(2)}) async-start(), calls=%async_computation.9 | async-start | bytes 2228224 | tf_op jit(solution)/shard_map/reduce_scatter | solution.py:34
  54.1 116.3 %reduce-scatter.8.cloned.1.call-start = ((), (), s32[]{:S(2)}) async-start(), calls=%async_computation.10 | async-start | bytes 196608 | tf_op jit(solution)/shard_map/reduce_scatter | solution.py:34
  159.4 9.0 %all-to-all-start.1 = ((f32[8,1,1]{2,1,0:T(1,128)}), f32[8,1,1]{2,1,0:T(1,128)S(1)}, u32[]{:S(2)}, u32[]{:S(2)}) async-start(f32[8,1,1]{2,1,0:T(1,128)} %broadcast_in_dim.8), calls=%async_computation.1 | async-start | bytes 8192 | tf_op jit(solution)/shard_map/all_to_all | solution.py:13
  170.4 13.1 %copy-start.1 = (f32[1,1,64,224]{3,2,0,1:T(8,128)S(1)}, f32[1,1,64,224]{3,2,0,1:T(8,128)}, u32[]{:S(2)}) copy-start(f32[1,1,64,224]{3,2,0,1:T(8,128)} %reduce-scatter.8.cloned.1.call-done) | copy-start | bytes 172036
  179.8 47.7 %all-to-all-start.3 = ((bf16[16,2,1,64,224]{4,3,1,2,0:T(8,128)(2,1)}), bf16[16,2,1,64,224]{4,3,1,2,0:T(8,128)(2,1)S(1)}, u32[]{:S(2)}, u32[]{:S(2)}) async-start(bf16[16,2,1,64,224]{4,3,1,2,0:T(8,128)(2,1)} %stack.10), calls=%async_computation.6 | async-start | bytes 2097152 | tf_op jit(solution)/shard_map/all_to_all | solution.py:63
Sparse Core Ops, SparseCore 0:
  24.9 29.1 reduce-scatter.3
  57.1 63.0 reduce-scatter.5
  123.1 30.0 reduce-scatter.7
